TPU v7x, 256 devices: a whole 4x4x8 slice. The times are simulated.
256 devices in a mesh: req: 16 (over z_hi, y, core), tp: 16 (over z_lo, x).
Axes of the slice: x: 4, y: 4, z: 8 (z_hi: 2, z_lo: 4; z = z_hi * 4 + z_lo), core: 2. Of those that a mesh axis runs over, the one named last changes fastest.
Arguments:
- queries: bfloat16 [64, 32, 4096], P('req'), may hold values from -128 to 128
- cache_keys: bfloat16 [64, 4096, 512], P('req', 'tp'), may hold values from -4 to 4
- cache_values: bfloat16 [64, 4096, 512], P('req', 'tp'), may hold values from -5 to 5
- tree_keys: bfloat16 [64, 32, 512], P('req', 'tp'), may hold values from -5 to 5
- tree_values: bfloat16 [64, 32, 512], P('req', 'tp'), may hold values from -5 to 5
- parents: int32 [64, 32], P('req'), may hold values from -1 to 30, as said below
- lengths: int32 [64], P('req'), may hold values from 2 to 4096
- accepted_leaf: int32 [64], P('req'), may hold values from 0 to 31
- residual: bfloat16 [64, 32, 8192], P('req', None, 'tp'), may hold values from -12 to 12
- norm_gain: float32 [8192], replicated, may hold values from 0.5 to 4
- out_weight: bfloat16 [4096, 8192], P('tp'), may hold values from -0.09375 to 0.09375
- prev_feature: bfloat16 [64, 8192], P('req'), may hold values from -5 to 5
- draft_weight: bfloat16 [8192, 8192], P('req', 'tp'), may hold values from -0.0625 to 0.0625
- first_moment: float32 [8192, 8192], P('req', 'tp'), may hold values from -5 to 5
- second_moment: float32 [8192, 8192], P('req', 'tp'), may hold values from 0.25 to 4
Outputs:
- features: bfloat16 [64, 32, 8192], P('req', None, 'tp')
- new_weight: bfloat16 [8192, 8192], P('req', 'tp')
- new_first: float32 [8192, 8192], P('req', 'tp')
- new_second: float32 [8192, 8192], P('req', 'tp')
- draft_loss: float32 [], replicated
Inputs may be any that keep to these rules, and one draw needn't show every extreme that they name: parents[r, 0] = -1; for i of 1 or more, parents[r, i] lies in 0 to i - 1; node 31 is a child of node 30.
All inputs are finite; a program needn't handle non-finite values.
Results may differ from a plain program's by a relative error of at most 0.014.
Values may be sent and summed in bfloat16 or wider, within the bound.
No kernel may reach another device: no remote copies, remote signals or barrier semaphores. Data moves between devices by JAX's collectives and lax.ppermute only.
A program may use at most 128 MiB of HBM per device.

v0:
```python
import math
import jax
import jax.numpy as jnp
from jax import lax
from jax.sharding import PartitionSpec as P

HEADS = 32
KV_HEADS = 4
HEAD = 128
NODES = 32
CACHE = 4096
NEG_FILL = -1e30
NORM_EPSILON = 1e-06
BETA_ONE = 0.9
BETA_TWO = 0.95
CORRECT_ONE = 1.0 - 0.9**10
CORRECT_TWO = 1.0 - 0.95**10
LEARN_RATE = 0.001


def closure(parents):
    node_count = parents.shape[-1]
    onehot = (parents[:, :, None] == jnp.arange(node_count, dtype=jnp.int32)[None, None, :]).astype(
        jnp.float32
    )
    reach_map = jnp.eye(node_count, dtype=jnp.float32)[None] + onehot
    for repeat in range(node_count.bit_length()):
        reach_map = jnp.minimum(
            jnp.einsum("rij,rjk->rik", reach_map, reach_map, precision=lax.Precision.HIGHEST), 1.0
        )
    return reach_map


def body(
    queries,
    cache_keys,
    cache_values,
    tree_keys,
    tree_values,
    parents,
    lengths,
    accepted_leaf,
    residual,
    norm_gain,
    out_weight,
    prev_feature,
    draft_weight,
    first_moment,
    second_moment,
):
    full_residual = lax.all_gather(residual, "tp", axis=2, tiled=True)
    requests = queries.shape[0]
    row_count = requests * NODES
    groups = HEADS // KV_HEADS
    score_scale = 1.0 / math.sqrt(HEAD)
    tp_rank = lax.axis_index("tp")
    cache_span = cache_keys.shape[1]
    tree_span = tree_keys.shape[1]
    reach_map = closure(parents)
    query_view = queries.reshape(requests, NODES, KV_HEADS, groups, HEAD)
    cache_view = cache_keys.reshape(requests, cache_span, KV_HEADS, HEAD)
    tree_view = tree_keys.reshape(requests, tree_span, KV_HEADS, HEAD)
    cache_scores = (
        jnp.einsum("rnkgd,rckd->rkgnc", query_view, cache_view, preferred_element_type=jnp.float32)
        * score_scale
    )
    tree_scores = (
        jnp.einsum("rnkgd,rjkd->rkgnj", query_view, tree_view, preferred_element_type=jnp.float32)
        * score_scale
    )
    positions = tp_rank * cache_span + jnp.arange(cache_span, dtype=jnp.int32)
    cache_live = (positions[None, :] < lengths[:, None])[:, None, None, None, :]
    visible = lax.dynamic_slice_in_dim(reach_map, tp_rank * tree_span, tree_span, 2)
    tree_live = (visible > 0.5)[:, None, None, :, :]
    cache_scores = jnp.where(cache_live, cache_scores, NEG_FILL)
    tree_scores = jnp.where(tree_live, tree_scores, NEG_FILL)
    local_top = jnp.maximum(jnp.max(cache_scores, axis=-1), jnp.max(tree_scores, axis=-1))
    row_top = lax.pmax(local_top, "tp")
    cache_probs = jnp.where(cache_live, jnp.exp(cache_scores - row_top[..., None]), 0.0).astype(
        jnp.bfloat16
    )
    tree_probs = jnp.where(tree_live, jnp.exp(tree_scores - row_top[..., None]), 0.0).astype(
        jnp.bfloat16
    )
    totals = jnp.sum(cache_probs, axis=-1, dtype=jnp.float32) + jnp.sum(
        tree_probs, axis=-1, dtype=jnp.float32
    )
    value_view = cache_values.reshape(requests, cache_span, KV_HEADS, HEAD)
    tree_value_view = tree_values.reshape(requests, tree_span, KV_HEADS, HEAD)
    weighted = jnp.einsum(
        "rkgnc,rckd->rnkgd", cache_probs, value_view, preferred_element_type=jnp.float32
    )
    weighted = weighted + jnp.einsum(
        "rkgnj,rjkd->rnkgd", tree_probs, tree_value_view, preferred_element_type=jnp.float32
    )
    weighted = weighted.reshape(row_count, HEADS * HEAD)
    totals = jnp.transpose(totals, (0, 3, 1, 2)).reshape(row_count, HEADS)
    head_sums, head_totals = (
        lax.psum_scatter(weighted, "tp", scatter_dimension=1, tiled=True),
        lax.psum_scatter(totals, "tp", scatter_dimension=1, tiled=True),
    )
    own_heads = head_totals.shape[1]
    attended = (head_sums.reshape(row_count, own_heads, HEAD) / head_totals[:, :, None]).astype(
        jnp.bfloat16
    )
    partial_value = jnp.dot(
        attended.reshape(row_count, own_heads * HEAD),
        out_weight,
        preferred_element_type=jnp.float32,
    )
    partial_value = lax.optimization_barrier(partial_value.astype(jnp.bfloat16)).astype(jnp.float32)
    model_width = partial_value.shape[1]
    block_width = model_width // lax.axis_size("tp")
    summed = lax.psum(partial_value.astype(jnp.bfloat16), "tp").astype(jnp.float32)
    mixed = full_residual.reshape(row_count, model_width).astype(jnp.float32) + summed
    mean_sq = jnp.mean(mixed * mixed, axis=1, keepdims=True)
    features = (mixed * lax.rsqrt(mean_sq + NORM_EPSILON) * norm_gain[None, :]).astype(jnp.bfloat16)
    own_block = lax.dynamic_slice_in_dim(features, tp_rank * block_width, block_width, 1)
    feature_table = jnp.concatenate(
        [prev_feature[:, None, :], features.reshape(requests, NODES, model_width)], axis=1
    )
    inputs = jnp.take_along_axis(feature_table, (parents + 1)[:, :, None], axis=1).reshape(
        row_count, model_width
    )
    leaf_hot = (accepted_leaf[:, None] == jnp.arange(NODES, dtype=jnp.int32)[None, :]).astype(
        jnp.float32
    )
    accepted = jnp.einsum("rn,rnj->rj", leaf_hot, reach_map, precision=lax.Precision.HIGHEST)
    fill_share = 0.5 + lengths.astype(jnp.float32) / CACHE
    weights = ((1.0 + 3.0 * accepted) * fill_share[:, None]).reshape(row_count, 1)
    columns = inputs
    predicted = jnp.dot(
        columns,
        lax.all_gather(draft_weight, "req", axis=0, tiled=True),
        preferred_element_type=jnp.float32,
    )
    pred_error = predicted - own_block.astype(jnp.float32)
    scaled_err = (weights * pred_error).astype(jnp.bfloat16)
    columns = inputs
    gradient = lax.psum_scatter(
        lax.dot_general(
            columns, scaled_err, (((0,), (0,)), ((), ())), preferred_element_type=jnp.float32
        ),
        "req",
        scatter_dimension=0,
        tiled=True,
    )
    square_total, error_total = lax.psum(
        (jnp.sum(gradient * gradient), jnp.sum(weights * pred_error * pred_error)), ("req", "tp")
    )
    draft_loss = 0.5 * error_total / (row_count * lax.axis_size("req") * model_width)
    grad_norm = jnp.sqrt(square_total) + 1e-06
    clip_factor = jnp.minimum(1.0, model_width / grad_norm)
    clipped = gradient * clip_factor
    new_first = BETA_ONE * first_moment + (1.0 - BETA_ONE) * clipped
    new_second = BETA_TWO * second_moment + (1.0 - BETA_TWO) * clipped * clipped
    direction = new_first / CORRECT_ONE / (jnp.sqrt(new_second / CORRECT_TWO) + 1e-08)
    new_weight = (draft_weight.astype(jnp.float32) - LEARN_RATE * direction).astype(jnp.bfloat16)
    return (
        own_block.reshape(requests, NODES, block_width),
        new_weight,
        new_first,
        new_second,
        draft_loss,
    )


def solution(mesh):
    placed = (
        P("req", None, None),
        P("req", "tp", None),
        P("req", "tp", None),
        P("req", "tp", None),
        P("req", "tp", None),
        P("req", None),
        P("req"),
        P("req"),
        P("req", None, "tp"),
        P(),
        P("tp", None),
        P("req", None),
        P("req", "tp"),
        P("req", "tp"),
        P("req", "tp"),
    )
    return jax.shard_map(
        body,
        mesh=mesh,
        in_specs=placed,
        out_specs=(P("req", None, "tp"), P("req", "tp"), P("req", "tp"), P("req", "tp"), P()),
        check_vma=False,
    )
```

profile of v0, /device:TPU:1, one launch (start us, length us, event | category | flops | bytes accessed | tf_op | source)
XLA Modules:
  0.0 868.4 jit_solution(2874297902461404456)
XLA Ops:
  7.3 1.1 convolution_minimum_fusion.4
  10.4 1.4 copy.89
  11.8 1.1 reshape.107
  13.3 1.5 fusion.38
  14.8 4.1 bitcast_reduce_fusion
  19.0 67.8 %pmax.7 = f32[4,4,8,32]{3,2,1,0:T(8,128)S(1)} all-reduce(f32[4,4,8,32]{3,2,1,0:T(8,128)S(1)} %max.5), channel_id=1, replica_groups=mesh['req'=16,'tp'=16] {'tp'}, use_global_device_ids=true, to_apply=%region_2.3 | all-reduce | flops 4096 | bytes 32768 | tf_op jit(solution)/shard_map/pmax | solution.py:78
  87.0 3.0 fusion.6
  90.0 0.5 add_bitcast_fusion
  90.5 1.2 copy.74
  91.7 1.5 reshape.112
  93.3 0.7 all-gather.3.cloned.1.call-update
  94.1 3.1 convert_reduce_fusion
  97.4 0.6 dynamic-slice
  98.6 61.0 %all-reduce = f32[128,32]{0,1:T(8,128)S(1)} all-reduce(f32[128,32]{0,1:T(8,128)S(1)} %reshape.113), channel_id=3, replica_groups=mesh['req'=16,'tp'=16] {'tp'}, use_global_device_ids=true, to_apply=%region_6.7.clone | all-reduce | flops 4096 | bytes 32768
  159.7 23.9 %reduce-scatter.3.cloned.1.call-done = f32[128,256]{1,0:T(8,128)} async-done(((f32[128,4096]{1,0:T(8,128)}), f32[128,256]{1,0:T(8,128)}) %reduce-scatter.3.cloned.1.call-update) | async-done | bytes 131088 | tf_op jit(solution)/shard_map/reduce_scatter | solution.py:99
  183.9 4.3 convolution_convert_fusion
  188.3 0.5 all-gather.5.cloned.1.call-update
  189.7 75.2 %all-gather.3.cloned.1.call-done = bf16[4,32,8192]{2,1,0:T(8,128)(2,1)} async-done(((bf16[4,32,512]{2,1,0:T(8,128)(2,1)}), bf16[4,32,8192]{2,1,0:T(8,128)(2,1)}) %all-gather.3.cloned.1.call-update) | async-done | bytes 2097168 | tf_op jit(solution)/shard_map/all_gather | solution.py:51
  264.8 168.2 %all-reduce.4.cloned.1.call-done = bf16[128,8192]{1,0:T(8,128)(2,1)} async-done(((bf16[128,8192]{1,0:T(8,128)(2,1)}), bf16[128,8192]{1,0:T(8,128)(2,1)}) %all-reduce.4.cloned.1.call-update) | async-done | bytes 2097168 | tf_op jit(solution)/shard_map/psum | solution.py:114
  433.0 3.1 multiply_reduce_fusion
  436.2 1.0 multiply_convert_fusion
  437.2 1.6 copy.77
  438.9 1.4 pad_maximum_fusion
  440.3 8.3 gather_fusion
  448.5 0.9 constant_dynamic-slice_fusion.1
  449.5 103.7 %all-gather.5.cloned.1.call-done = bf16[8192,512]{1,0:T(8,128)(2,1)} async-done(((bf16[512,512]{1,0:T(8,128)(2,1)}), bf16[8192,512]{1,0:T(8,128)(2,1)}) %all-gather.5.cloned.1.call-update) | async-done | bytes 8388624 | tf_op jit(solution)/shard_map/all_gather | solution.py:134
  553.2 6.2 fusion.13
  559.4 8.2 fusion.12
  567.6 210.0 %reduce-scatter.5.cloned.1.call-done = f32[512,512]{1,0:T(8,128)} async-done(((f32[8192,512]{1,0:T(8,128)}), f32[512,512]{1,0:T(8,128)}) %reduce-scatter.5.cloned.1.call-update) | async-done | bytes 1048592 | tf_op jit(solution)/shard_map/reduce_scatter | solution.py:140
  777.6 2.1 multiply_reduce_fusion.1
  779.7 76.2 %all-reduce.1 = (f32[]{:T(128)}, f32[]{:T(128)}) all-reduce(f32[]{:T(128)} %multiply_reduce_fusion.1, f32[]{:T(128)} %get-tuple-element.16), channel_id=1, replica_groups=mesh['req'=16,'tp'=16] {'req','tp'}, use_global_device_ids=true, to_apply=%region_11.12 | all-reduce | flops 2 | bytes 16 | tf_op jit(solution)/shard_map/psum | solution.py:148
  857.3 3.4 subtract_convert_fusion
  (81 shorter events, 4.1 us)
Async XLA Ops:
  7.2 82.8 %copy-start = (bf16[4,2,512]{2,1,0:T(2,128)(2,1)S(1)}, bf16[4,2,512]{2,1,0:T(2,128)(2,1)}, u32[]{:S(2)}) copy-start(bf16[4,2,512]{2,1,0:T(2,128)(2,1)} %param.19) | copy-start | bytes 24580
  7.2 4.7 copy-start.9
  7.2 5.8 copy-start.10
  7.2 6.0 copy-start.15
  7.2 6.1 copy-start.16
  7.2 176.4 %reduce-scatter.3.cloned.1.call-start = ((), (), s32[]{:S(2)}) async-start(), calls=%async_computation.3 | async-start | bytes 2228224 | tf_op jit(solution)/shard_map/reduce_scatter | solution.py:99
  93.2 4.2 copy-start.18
  93.3 171.5 %all-gather.3.cloned.1.call-start = ((), (), s32[]{:S(2)}) async-start(), calls=%async_computation.2 | async-start | bytes 2228224 | tf_op jit(solution)/shard_map/all_gather | solution.py:51
  94.0 338.9 %all-reduce.4.cloned.1.call-start = ((), (), s32[]{:S(2)}) async-start(), calls=%async_computation.4 | async-start | bytes 4194304 | tf_op jit(solution)/shard_map/psum | solution.py:114
  183.9 5.2 copy-start.14
  183.9 5.4 copy-start.17
  188.2 247.9 %copy-start.13 = (f32[8192]{0:T(1024)S(1)}, f32[8192]{0:T(1024)}, u32[]{:S(2)}) copy-start(f32[8192]{0:T(1024)} %param.24) | copy-start | bytes 98308
  188.2 365.0 %all-gather.5.cloned.1.call-start = ((), (), s32[]{:S(2)}) async-start(), calls=%async_computation.5 | async-start | bytes 8912896 | tf_op jit(solution)/shard_map/all_gather | solution.py:134
  188.8 588.8 %reduce-scatter.5.cloned.1.call-start = ((), (), s32[]{:S(2)}) async-start(), calls=%async_computation.6 | async-start | bytes 17825792 | tf_op jit(solution)/shard_map/reduce_scatter | solution.py:140
  264.8 171.3 %copy-start.4 = (bf16[4,32,8192]{2,1,0:T(8,128)(2,1)S(1)}, bf16[4,32,8192]{2,1,0:T(8,128)(2,1)}, u32[]{:S(2)}) copy-start(bf16[4,32,8192]{2,1,0:T(8,128)(2,1)} %all-gather.3.cloned.1.call-done) | copy-start | bytes 6291460
  433.0 3.2 copy-start.5
  436.1 2.7 copy-start.12
  437.2 1.6 copy-start.3
  449.5 109.9 %copy-start.11 = (bf16[128,512]{1,0:T(8,128)(2,1)}, bf16[128,512]{1,0:T(8,128)(2,1)S(1)}, u32[]{:S(2)}) copy-start(bf16[128,512]{1,0:T(8,128)(2,1)S(1)} %constant_dynamic-slice_fusion.1) | copy-start | bytes 393220
  449.5 109.9 %copy-start.2 = (bf16[128,8192]{1,0:T(8,128)(2,1)S(1)}, bf16[128,8192]{1,0:T(8,128)(2,1)}, u32[]{:S(2)}) copy-start(bf16[128,8192]{1,0:T(8,128)(2,1)} %gather_fusion) | copy-start | bytes 6291460
  567.6 289.7 %copy-start.6 = (bf16[512,512]{1,0:T(8,128)(2,1)S(1)}, bf16[512,512]{1,0:T(8,128)(2,1)}, u32[]{:S(2)}) copy-start(bf16[512,512]{1,0:T(8,128)(2,1)} %param.27) | copy-start | bytes 1572868
  567.6 289.7 %copy-start.7 = (f32[512,512]{1,0:T(8,128)S(1)}, f32[512,512]{1,0:T(8,128)}, u32[]{:S(2)}) copy-start(f32[512,512]{1,0:T(8,128)} %param.28) | copy-start | bytes 3145732
  567.6 289.7 %copy-start.8 = (f32[512,512]{1,0:T(8,128)S(1)}, f32[512,512]{1,0:T(8,128)}, u32[]{:S(2)}) copy-start(f32[512,512]{1,0:T(8,128)} %param.29) | copy-start | bytes 3145732
  567.6 293.1 %copy-start.1 = (bf16[4,2,512]{2,1,0:T(2,128)(2,1)S(1)}, bf16[4,2,512]{2,1,0:T(2,128)(2,1)}, u32[]{:S(2)}) copy-start(bf16[4,2,512]{2,1,0:T(2,128)(2,1)} %param.19) | copy-start | bytes 24580
Sparse Core Ops, SparseCore 0:
  93.4 90.2 reduce-scatter.2
  185.5 79.3 all-gather.2
  267.5 165.4 all-reduce.3
  435.6 117.5 all-gather.4
  567.7 209.8 reduce-scatter.4
where the time goes:
time: 869 us; the launch traced here: 868 us
  waiting for transfers between devices  582 us (67%)
  blocking collectives  205 us (24%)
  matrix products  30.4 us (3%)
  local copies, waits for them, and re-layouts  18.2 us (2%)
  between operations  17.4 us (2%)
  other arithmetic  14.8 us (2%)
    reduce_scatter x1, waiting for transfers between devices, body(): lax.psum_scatter(lax.dot_general(columns, scaled_err, (((0,), (0,)), ((),...  210 us
    psum x1, waiting for transfers between devices, body(): lax.psum(partial_value.astype(jnp.bfloat16), 'tp').astype(jnp.float32)  168 us
    all_gather x1, waiting for transfers between devices, body(): lax.all_gather(draft_weight, 'req', axis=0, tiled=True)  104 us
    psum x1, blocking collectives, body(): lax.psum((jnp.sum(gradient * gradient), jnp.sum(weights * pred_error * pr...  76.2 us
    all_gather x1, waiting for transfers between devices, body(): full_residual = lax.all_gather(residual, 'tp', axis=2, tiled=True)  75.2 us
    pmax x1, blocking collectives, body(): row_top = lax.pmax(local_top, 'tp')  67.8 us
    unnamed x1, blocking collectives  61 us
    reduce_scatter x1, waiting for transfers between devices, body(): lax.psum_scatter(weighted, 'tp', scatter_dimension=1, tiled=True)  23.9 us
  transfers between devices with their start and end apart: 5, of which 5 were waited for; matrix products, arithmetic and copies ran while one was open for 3% of the time, Pallas kernels for 0%

commit v1 on v0

--- a/solution.py
+++ b/solution.py
@@ -48,7 +48,9 @@
     first_moment,
     second_moment,
 ):
-    full_residual = lax.all_gather(residual, "tp", axis=2, tiled=True)
+    full_residual = jnp.concatenate(
+        lax.all_to_all(jnp.stack([residual] * lax.axis_size("tp")), "tp", 0, 0), axis=2
+    )
     requests = queries.shape[0]
     row_count = requests * NODES
     groups = HEADS // KV_HEADS

time: 869 us -> 764 us (0.88)
  waiting for transfers between devices: 582 us -> 462 us
  local copies, waits for them, and re-layouts: 18.2 us -> 28.1 us
    all_gather x1, waiting for transfers between devices: 104 us -> 0.03 us  [body(): lax.all_gather(draft_weight, 'req', axis=0, tiled=True)]
    all_gather x1 -> x0, waiting for transfers between devices: 75.2 us -> none  [body(): full_residual = lax.all_gather(residual, 'tp', axis=2, tiled=True)]
    all_to_all x0 -> x1, waiting for transfers between devices: none -> 51.8 us  [body(): lax.all_to_all(jnp.stack([residual] * lax.axis_size('tp')), 'tp', 0, 0)]
    reduce_scatter x1, waiting for transfers between devices: 210 us -> 224 us  [body(): lax.psum_scatter(lax.dot_general(columns, scaled_err, (((0,), (0,)), ((),...]
  transfers between devices with their start and end apart: 5 -> 5, of which waited for: 5 -> 4; matrix products, arithmetic and copies ran while one was open for 3% -> 4% of each run, Pallas kernels for 0% -> 0%
where the time goes in v1:
time: 764 us; the launch traced here: 763 us
  waiting for transfers between devices  462 us (60%)
  blocking collectives  205 us (27%)
  matrix products  29 us (4%)
  local copies, waits for them, and re-layouts  28.1 us (4%)
  between operations  19.1 us (3%)
  other arithmetic  15.5 us (2%)
    reduce_scatter x1, waiting for transfers between devices, body(): lax.psum_scatter(lax.dot_general(columns, scaled_err, (((0,), (0,)), ((),...  224 us
    psum x1, waiting for transfers between devices, body(): lax.psum(partial_value.astype(jnp.bfloat16), 'tp').astype(jnp.float32)  161 us
    psum x1, blocking collectives, body(): lax.psum((jnp.sum(gradient * gradient), jnp.sum(weights * pred_error * pr...  76.3 us
    pmax x1, blocking collectives, body(): row_top = lax.pmax(local_top, 'tp')  67.8 us
    unnamed x1, blocking collectives  61.4 us
    all_to_all x1, waiting for transfers between devices, body(): lax.all_to_all(jnp.stack([residual] * lax.axis_size('tp')), 'tp', 0, 0)  51.8 us
    reduce_scatter x1, waiting for transfers between devices, body(): lax.psum_scatter(weighted, 'tp', scatter_dimension=1, tiled=True)  24.4 us
  transfers between devices with their start and end apart: 5, of which 4 were waited for; matrix products, arithmetic and copies ran while one was open for 4% of the time, Pallas kernels for 0%

profile of v1, /device:TPU:1, one launch (start us, length us, event | category | flops | bytes accessed | tf_op | source)
XLA Modules:
  0.0 763.3 jit_solution(13286843295787321085)
XLA Ops:
  8.1 1.1 convolution_minimum_fusion.4
  11.1 1.4 copy.92
  13.0 1.5 fusion.38
  14.5 2.9 bitcast_reduce_fusion
  17.4 67.8 %pmax.7 = f32[4,4,8,32]{3,2,1,0:T(8,128)S(1)} all-reduce(f32[4,4,8,32]{3,2,1,0:T(8,128)S(1)} %max.5), channel_id=1, replica_groups=mesh['req'=16,'tp'=16] {'tp'}, use_global_device_ids=true, to_apply=%region_2.3 | all-reduce | flops 4096 | bytes 32768 | tf_op jit(solution)/shard_map/pmax | solution.py:80
  85.7 2.9 fusion.6
  89.2 1.2 copy.76
  90.4 1.5 reshape.114
  92.0 3.1 convert_reduce_fusion
  95.4 0.6 dynamic-slice
  96.6 61.4 %all-reduce = f32[128,32]{0,1:T(8,128)S(1)} all-reduce(f32[128,32]{0,1:T(8,128)S(1)} %reshape.115), channel_id=3, replica_groups=mesh['req'=16,'tp'=16] {'tp'}, use_global_device_ids=true, to_apply=%region_6.7.clone | all-reduce | flops 4096 | bytes 32768
  158.1 24.4 %reduce-scatter.3.cloned.1.call-done = f32[128,256]{1,0:T(8,128)} async-done(((f32[128,4096]{1,0:T(8,128)}), f32[128,256]{1,0:T(8,128)}) %reduce-scatter.3.cloned.1.call-update) | async-done | bytes 131088 | tf_op jit(solution)/shard_map/reduce_scatter | solution.py:101
  182.8 4.3 convolution_convert_fusion
  187.7 1.6 stack.2
  189.3 3.7 all-to-all-start
  193.9 51.8 %all-to-all-done = bf16[16,4,32,512]{3,2,1,0:T(8,128)(2,1)S(1)} async-done(((bf16[16,4,32,512]{3,2,1,0:T(8,128)(2,1)}), bf16[16,4,32,512]{3,2,1,0:T(8,128)(2,1)S(1)}, u32[]{:S(2)}, u32[]{:S(2)}) %all-to-all-start) | async-done | bytes 2097184 | tf_op jit(solution)/shard_map/all_to_all | solution.py:52
  246.3 2.4 copy.52
  248.8 5.4 copy.91
  254.2 160.8 %all-reduce.4.cloned.1.call-done = bf16[128,8192]{1,0:T(8,128)(2,1)} async-done(((bf16[128,8192]{1,0:T(8,128)(2,1)}), bf16[128,8192]{1,0:T(8,128)(2,1)}) %all-reduce.4.cloned.1.call-update) | async-done | bytes 2097168 | tf_op jit(solution)/shard_map/psum | solution.py:116
  415.0 3.6 multiply_reduce_fusion
  419.1 0.7 copy-done.5
  419.7 0.7 multiply_convert_fusion
  420.5 1.6 copy.79
  422.1 1.4 pad_maximum_fusion
  423.5 8.5 %gather_fusion = bf16[128,8192]{1,0:T(8,128)(2,1)} fusion(bf16[4,33,8192]{2,0,1:T(4,128)(2,1)S(1)} %pad_maximum_fusion, s32[128]{0:T(128)S(1)} %reshape.119), kind=kCustom, calls=%fused_computation | custom fusion | bytes 4195328 | tf_op jit(solution)/shard_map/jit(take_along_axis)/gather | solution.py:124
  432.0 0.9 constant_dynamic-slice_fusion.1
  433.0 6.1 fusion.13
  439.1 8.2 %fusion.12 = f32[8192,512]{1,0:T(8,128)} fusion(bf16[128,8192]{1,0:T(8,128)(2,1)S(1)} %copy-done.3, pred[128]{0:T(512)(128)(4,1)S(1)} %broadcast_in_dim.74, f32[128,512]{1,0:T(8,128)S(1)} %get-tuple-element.17, f32[128]{0:T(128)S(1)} %mul.137), kind=kOutput, calls=%fused_computation.36 | convolution fusion | flops 1074921472 | bytes 19137152 | tf_op jit(solution)/shard_map/dot_general | solution.py:143
  447.3 224.3 %reduce-scatter.5.cloned.1.call-done = f32[512,512]{1,0:T(8,128)} async-done(((f32[8192,512]{1,0:T(8,128)}), f32[512,512]{1,0:T(8,128)}) %reduce-scatter.5.cloned.1.call-update) | async-done | bytes 1048592 | tf_op jit(solution)/shard_map/reduce_scatter | solution.py:142
  671.6 2.1 multiply_reduce_fusion.1
  673.7 76.3 %all-reduce.1 = (f32[]{:T(128)}, f32[]{:T(128)}) all-reduce(f32[]{:T(128)} %multiply_reduce_fusion.1, f32[]{:T(128)} %get-tuple-element.16), channel_id=1, replica_groups=mesh['req'=16,'tp'=16] {'req','tp'}, use_global_device_ids=true, to_apply=%region_11.12 | all-reduce | flops 2 | bytes 16 | tf_op jit(solution)/shard_map/psum | solution.py:150
  751.3 3.4 subtract_convert_fusion
  (86 shorter events, 6.4 us)
Async XLA Ops:
  8.0 80.7 %copy-start = (bf16[4,2,512]{2,1,0:T(2,128)(2,1)S(1)}, bf16[4,2,512]{2,1,0:T(2,128)(2,1)}, u32[]{:S(2)}) copy-start(bf16[4,2,512]{2,1,0:T(2,128)(2,1)} %param.19) | copy-start | bytes 24580
  8.0 4.6 copy-start.9
  8.0 4.9 copy-start.16
  8.0 5.0 copy-start.17
  8.0 174.5 %reduce-scatter.3.cloned.1.call-start = ((), (), s32[]{:S(2)}) async-start(), calls=%async_computation.3 | async-start | bytes 2228224 | tf_op jit(solution)/shard_map/reduce_scatter | solution.py:101
  13.0 72.2 %copy-start.10 = (bf16[4,256,512]{2,1,0:T(8,128)(2,1)S(1)}, bf16[4,256,512]{2,1,0:T(8,128)(2,1)}, u32[]{:S(2)}) copy-start(bf16[4,256,512]{2,1,0:T(8,128)(2,1)} %param.17) | copy-start | bytes 3145732
  92.0 3.4 copy-start.19
  92.0 323.0 %all-reduce.4.cloned.1.call-start = ((), (), s32[]{:S(2)}) async-start(), calls=%async_computation.4 | async-start | bytes 4194304 | tf_op jit(solution)/shard_map/psum | solution.py:116
  182.7 5.0 copy-start.11
  187.1 6.2 copy-start.15
  187.1 6.3 copy-start.18
  187.1 245.8 %all-gather.2.cloned.1.call-start = ((), (), s32[]{:S(2)}) async-start(), calls=%async_computation.5 | async-start | bytes 8912896 | tf_op jit(solution)/shard_map/all_gather | solution.py:136
  189.3 56.4 %all-to-all-start = ((bf16[16,4,32,512]{3,2,1,0:T(8,128)(2,1)}), bf16[16,4,32,512]{3,2,1,0:T(8,128)(2,1)S(1)}, u32[]{:S(2)}, u32[]{:S(2)}) async-start(bf16[16,4,32,512]{3,2,1,0:T(8,128)(2,1)} %stack.2), calls=%async_computation | async-start | bytes 4194304 | tf_op jit(solution)/shard_map/all_to_all | solution.py:52
  193.1 478.5 %reduce-scatter.5.cloned.1.call-start = ((), (), s32[]{:S(2)}) async-start(), calls=%async_computation.6 | async-start | bytes 17825792 | tf_op jit(solution)/shard_map/reduce_scatter | solution.py:142
  248.8 169.9 %copy-start.14 = (f32[8192]{0:T(1024)S(1)}, f32[8192]{0:T(1024)}, u32[]{:S(2)}) copy-start(f32[8192]{0:T(1024)} %param.24) | copy-start | bytes 98308
  415.0 4.1 copy-start.2
  415.0 4.7 copy-start.5
  420.4 1.7 copy-start.4
  420.4 1.7 copy-start.13
  432.9 6.2 copy-start.12
  432.9 6.2 copy-start.3
  447.3 304.1 %copy-start.6 = (bf16[512,512]{1,0:T(8,128)(2,1)S(1)}, bf16[512,512]{1,0:T(8,128)(2,1)}, u32[]{:S(2)}) copy-start(bf16[512,512]{1,0:T(8,128)(2,1)} %param.27) | copy-start | bytes 1572868
  447.3 304.1 %copy-start.7 = (f32[512,512]{1,0:T(8,128)S(1)}, f32[512,512]{1,0:T(8,128)}, u32[]{:S(2)}) copy-start(f32[512,512]{1,0:T(8,128)} %param.28) | copy-start | bytes 3145732
  447.3 304.1 %copy-start.8 = (f32[512,512]{1,0:T(8,128)S(1)}, f32[512,512]{1,0:T(8,128)}, u32[]{:S(2)}) copy-start(f32[512,512]{1,0:T(8,128)} %param.29) | copy-start | bytes 3145732
  447.3 307.4 %copy-start.1 = (bf16[4,2,512]{2,1,0:T(2,128)(2,1)S(1)}, bf16[4,2,512]{2,1,0:T(2,128)(2,1)}, u32[]{:S(2)}) copy-start(bf16[4,2,512]{2,1,0:T(2,128)(2,1)} %param.19) | copy-start | bytes 24580
Sparse Core Ops, SparseCore 0:
  92.1 90.3 reduce-scatter.2
  187.2 227.7 all-reduce.3
Sparse Core Ops, SparseCore 1:
  190.3 98.2 all-gather.1
  447.4 224.1 reduce-scatter.4
